TPU v7x, 32 devices: a whole 2x2x4 slice. The times are simulated.
32 devices in a mesh: rep: 8 (over y, x, core), tp: 4 (over z).
Axes of the slice: x: 2, y: 2, z: 4, core: 2. Of those that a mesh axis runs over, the one named last changes fastest.
Arguments:
- context: bfloat16 [16384, 5120], P('rep', 'tp'), may hold values from -6 to 6
- out_grad: bfloat16 [16384, 5120], P('rep', 'tp'), may hold values from -6 to 6
- rewards: int32 [8, 32], P(None, 'rep'), may hold values from 0 to 1
- master: float32 [5120, 5120], P('rep', 'tp'), may hold values from -0.078125 to 0.078125
- first_moment: float32 [5120, 5120], P('rep', 'tp'), may hold values from -0.046875 to 0.046875
- second_moment: float32 [5120, 5120], P('rep', 'tp'), may hold values from 6.1035155e-07 to 6.1035156e-05
- inputs: bfloat16 [4, 256, 5120], P(None, 'rep'), may hold values from -6 to 6
- w_query: bfloat16 [5120, 5120], P(None, 'tp'), may hold values from -0.078125 to 0.078125
- w_key: bfloat16 [5120, 1024], P(None, 'tp'), may hold values from -0.078125 to 0.078125
- w_value: bfloat16 [5120, 1024], P(None, 'tp'), may hold values from -0.078125 to 0.078125
- cache_keys: bfloat16 [256, 256, 1024], P('rep', None, 'tp'), may hold values from -400 to 400
- cache_values: bfloat16 [256, 256, 1024], P('rep', None, 'tp'), may hold values from -24 to 24
- lengths: int32 [32], P('rep'), may hold values from 64 to 256
Outputs:
- decoded: bfloat16 [4, 256, 5120], P(None, 'rep')
- adam_step: float32 [5120, 5120], P('rep', 'tp')
All inputs are finite; a program needn't handle non-finite values.
Results may differ from a plain program's by a relative error of at most 0.0088.
Values may be sent and summed in bfloat16 or wider, within the bound.
No kernel may reach another device: no remote copies, remote signals or barrier semaphores. Data moves between devices by JAX's collectives and lax.ppermute only.
A program may use at most 192 MiB of HBM per device.

v0:
```python
import jax
import jax.numpy as jnp
from jax import lax
from jax.sharding import PartitionSpec as P

HEAD_DIM = 128
rope_base = 1000000.0
first_beta = 0.9
second_beta = 0.95
adam_epsilon = 1e-08
step_count = 10
learn_rate = 0.001


def rotate(vectors, positions):
    half_dim = vectors.shape[-1] // 2
    frequency = rope_base ** (-2.0 * jnp.arange(half_dim, dtype=jnp.float32) / vectors.shape[-1])
    angles = positions[..., None].astype(jnp.float32) * frequency
    cosine_table = jnp.cos(angles)
    sine_table = jnp.sin(angles)
    former = vectors[..., :half_dim]
    latter = vectors[..., half_dim:]
    return jnp.concatenate(
        [former * cosine_table - latter * sine_table, latter * cosine_table + former * sine_table],
        axis=-1,
    )


def attend(queries, old_keys, old_values, new_keys, new_values, live_mask):
    score_scale = HEAD_DIM ** (-0.5)
    step_total = queries.shape[0]
    cache_scores = (
        jnp.einsum("tsgqd,scgd->tsgqc", queries, old_keys, preferred_element_type=jnp.float32)
        * score_scale
    )
    cache_scores = jnp.where(live_mask[None, :, None, None, :], cache_scores, -1e30)
    recent = (
        jnp.einsum("tsgqd,usgd->tsgqu", queries, new_keys, preferred_element_type=jnp.float32)
        * score_scale
    )
    causal = jnp.arange(step_total)[:, None] >= jnp.arange(step_total)[None, :]
    recent = jnp.where(causal[:, None, None, None, :], recent, -1e30)
    row_peak = jnp.maximum(jnp.max(cache_scores, axis=-1), jnp.max(recent, axis=-1))[..., None]
    cache_exp = jnp.exp(cache_scores - row_peak)
    recent_exp = jnp.exp(recent - row_peak)
    denominator = jnp.sum(cache_exp, axis=-1, keepdims=True) + jnp.sum(
        recent_exp, axis=-1, keepdims=True
    )
    cache_weight = (cache_exp / denominator).astype(jnp.bfloat16)
    recent_weight = (recent_exp / denominator).astype(jnp.bfloat16)
    attended = jnp.einsum(
        "tsgqc,scgd->tsgqd", cache_weight, old_values, preferred_element_type=jnp.float32
    )
    attended = attended + jnp.einsum(
        "tsgqu,usgd->tsgqd", recent_weight, new_values, preferred_element_type=jnp.float32
    )
    return attended.astype(jnp.bfloat16)


def per_device(
    context,
    out_grad,
    rewards,
    master,
    first_moment,
    second_moment,
    inputs,
    w_query,
    w_key,
    w_value,
    cache_keys,
    cache_values,
    lengths,
):
    replicas = lax.axis_size("rep")
    prompt_count, local_group = rewards.shape
    totals = lax.psum(jnp.sum(rewards, axis=1), "rep")
    group_size = local_group * replicas
    advantage = rewards.astype(jnp.float32) - totals.astype(jnp.float32)[:, None] / group_size
    token_local = context.shape[0]
    per_token = jnp.repeat(advantage.reshape(-1), token_local // (prompt_count * local_group)) / (
        token_local * replicas
    )
    scaled = (out_grad.astype(jnp.float32) * per_token[:, None]).astype(jnp.bfloat16)
    features = lax.all_gather(context, "tp", axis=1, tiled=True)
    gradient = lax.psum_scatter(
        lax.dot_general(
            features, scaled, (((0,), (0,)), ((), ())), preferred_element_type=jnp.float32
        ).astype(jnp.bfloat16),
        "rep",
        scatter_dimension=0,
        tiled=True,
    ).astype(jnp.float32)
    moment_new = first_beta * first_moment + (1.0 - first_beta) * gradient
    square_new = second_beta * second_moment + (1.0 - second_beta) * gradient * gradient
    adam_step = (
        moment_new
        / (1.0 - first_beta**step_count)
        / (jnp.sqrt(square_new / (1.0 - second_beta**step_count)) + adam_epsilon)
    )
    weight = (master - learn_rate * adam_step).astype(jnp.bfloat16)
    step_total, seq_local, model_width = inputs.shape
    local_heads = w_query.shape[1] // HEAD_DIM
    local_kv = w_key.shape[1] // HEAD_DIM
    flat_rows = inputs.reshape(step_total * seq_local, model_width)
    queries = jnp.dot(flat_rows, w_query, preferred_element_type=jnp.float32).reshape(
        step_total, seq_local, local_heads, HEAD_DIM
    )
    key_new = jnp.dot(flat_rows, w_key, preferred_element_type=jnp.float32).reshape(
        step_total, seq_local, local_kv, HEAD_DIM
    )
    value_new = (
        jnp.dot(flat_rows, w_value, preferred_element_type=jnp.float32)
        .reshape(step_total, seq_local, local_kv, HEAD_DIM)
        .astype(jnp.bfloat16)
    )
    seq_length = jnp.repeat(lengths, seq_local // lengths.shape[0])
    positions = seq_length[None, :] + jnp.arange(step_total, dtype=jnp.int32)[:, None]
    queries = rotate(queries, positions[:, :, None]).astype(jnp.bfloat16)
    queries = queries.reshape(step_total, seq_local, local_kv, local_heads // local_kv, HEAD_DIM)
    key_new = rotate(key_new, positions[:, :, None]).astype(jnp.bfloat16)
    slot_total = cache_keys.shape[1]
    old_keys = cache_keys.reshape(seq_local, slot_total, local_kv, HEAD_DIM)
    old_values = cache_values.reshape(seq_local, slot_total, local_kv, HEAD_DIM)
    live_mask = jnp.arange(slot_total, dtype=jnp.int32)[None, :] < seq_length[:, None]
    attended = attend(queries, old_keys, old_values, key_new, value_new, live_mask)
    attended = attended.reshape(step_total * seq_local, local_heads * HEAD_DIM)
    all_heads = lax.all_gather(attended, "tp", axis=1, tiled=True)
    feature_rows = lax.all_to_all(all_heads, "rep", split_axis=1, concat_axis=0, tiled=True)
    own_columns = lax.psum_scatter(
        jnp.dot(feature_rows, weight, preferred_element_type=jnp.float32),
        "rep",
        scatter_dimension=0,
        tiled=True,
    )
    decoded = lax.all_gather(own_columns.astype(jnp.bfloat16), "tp", axis=1, tiled=True)
    return (decoded.reshape(step_total, seq_local, model_width), adam_step)


def solution(mesh):
    placed = (
        P("rep", "tp"),
        P("rep", "tp"),
        P(None, "rep"),
        P("rep", "tp"),
        P("rep", "tp"),
        P("rep", "tp"),
        P(None, "rep", None),
        P(None, "tp"),
        P(None, "tp"),
        P(None, "tp"),
        P("rep", None, "tp"),
        P("rep", None, "tp"),
        P("rep"),
    )
    return jax.shard_map(
        per_device,
        mesh=mesh,
        in_specs=placed,
        out_specs=(P(None, "rep", None), P("rep", "tp")),
        check_vma=False,
    )
```

profile of v0, /device:TPU:0, one launch (start us, length us, event | category | flops | bytes accessed | tf_op | source)
XLA Modules:
  0.0 632.1 jit_solution(17506920975322697041)
XLA Ops:
  8.1 4.4 copy.64
  12.5 4.5 copy.69
  17.0 7.3 %reshape.131 = bf16[32,256,2,128]{3,2,1,0:T(2,128)(2,1)} reshape(bf16[32,256,256]{2,1,0:T(8,128)(2,1)} %param.23) | data formatting | bytes 8388608 | tf_op jit(solution)/shard_map/reshape | solution.py:123
  24.3 7.2 %reshape.132 = bf16[32,256,2,128]{3,2,1,0:T(2,128)(2,1)} reshape(bf16[32,256,256]{2,1,0:T(8,128)(2,1)} %param.24) | data formatting | bytes 8388608 | tf_op jit(solution)/shard_map/reshape | solution.py:124
  31.5 17.8 %copy.41 = bf16[5120,1280]{0,1:T(8,128)(2,1)} copy(bf16[5120,1280]{1,0:T(8,128)(2,1)} %param.20) | data formatting | bytes 26214400 | tf_op args[7]
  49.6 7.2 %fusion.27 = f32[4,32,10,128]{3,1,2,0:T(8,128)S(1)} fusion(bf16[10,128,5120,1]{2,1,0,3:T(8,128)(2,1)} %bitcast.73, bf16[4,32,5120]{2,1,0:T(8,128)(2,1)S(1)} %copy-done), kind=kOutput, calls=%fused_computation.34 | convolution fusion | flops 1677721600 | bytes 15073280 | tf_op jit(solution)/shard_map/dot_general | solution.py:106
  57.5 1.1 copy-done.5
  58.6 1.0 fusion.25
  59.9 2.6 fusion.55
  62.5 1.6 bitcast_reduce_fusion
  64.6 1.3 fusion.16
  66.0 1.0 fusion.37
  68.2 1.5 fusion.29
  69.7 1.1 reshape.133
  70.9 9.6 %psum.7 = s32[8]{0:T(128)S(1)} all-reduce(s32[8]{0:T(128)S(1)} %reduce_sum.29), channel_id=1, replica_groups=mesh['rep'=8,'tp'=4] {'rep'}, use_global_device_ids=true, to_apply=%region_5.6 | all-reduce | flops 8 | bytes 64 | tf_op jit(solution)/shard_map/psum | solution.py:77
  80.9 288.3 %all-gather.6.cloned.1.call-done = bf16[2048,5120]{1,0:T(8,128)(2,1)} async-done(((bf16[2048,1280]{1,0:T(8,128)(2,1)}), bf16[2048,5120]{1,0:T(8,128)(2,1)}) %all-gather.6.cloned.1.call-update) | async-done | bytes 20971536 | tf_op jit(solution)/shard_map/all_gather | solution.py:85
  369.1 34.5 %fusion = bf16[5120,1280]{0,1:T(8,128)(2,1)} fusion(bf16[2048,5120]{1,0:T(8,128)(2,1)} %all-gather.6.cloned.1.call-done, bf16[2048,1280]{1,0:T(8,128)(2,1)} %param.14, f32[2048]{0:T(1024)S(1)} %div.60), kind=kOutput, calls=%fused_computation.1 | convolution fusion | flops 26857963520 | bytes 39329792 | tf_op jit(solution)/shard_map/dot_general | solution.py:87
  403.7 17.6 %copy.72 = bf16[5120,1280]{1,0:T(8,128)(2,1)} copy(bf16[5120,1280]{0,1:T(8,128)(2,1)} %fusion) | data formatting | bytes 26214400
  421.4 2.5 copy.94
  423.9 3.7 all-to-all-start
  427.6 4.9 copy.55
  432.5 5.1 copy.52
  437.5 4.8 copy.54
  442.3 72.5 %reduce-scatter.7.cloned.1.call-done = bf16[640,1280]{1,0:T(8,128)(2,1)} async-done(((bf16[5120,1280]{1,0:T(8,128)(2,1)}), bf16[640,1280]{1,0:T(8,128)(2,1)}) %reduce-scatter.7.cloned.1.call-update) | async-done | bytes 1638416
  514.8 2.8 copy.73
  517.6 6.7 %fusion.8 = f32[640,1280]{0,1:T(8,128)} fusion(bf16[640,1280]{0,1:T(8,128)(2,1)S(1)} %copy.73, f32[640,1280]{0,1:T(8,128)} %copy.54, f32[640,1280]{0,1:T(8,128)} %copy.52), kind=kLoop, calls=%fused_computation.12 | loop fusion | flops 9830400 | bytes 11468800 | tf_op jit(solution)/shard_map/div | solution.py:97
  524.4 7.5 %fusion.14 = f32[1024,1280]{1,0:T(8,128)} fusion(bf16[1024,640]{1,0:T(8,128)(2,1)S(1)} %bitcast.74, f32[640,1280]{0,1:T(8,128)} %copy.55, f32[640,1280]{0,1:T(8,128)} %fusion.8), kind=kOutput, calls=%fused_computation.23 | convolution fusion | flops 1680179200 | bytes 13107200 | tf_op jit(solution)/shard_map/dot_general | solution.py:131
  531.9 56.6 %reduce-scatter.5.cloned.1.call-done = f32[128,1280]{1,0:T(8,128)} async-done(((f32[1024,1280]{1,0:T(8,128)}), f32[128,1280]{1,0:T(8,128)}) %reduce-scatter.5.cloned.1.call-update) | async-done | bytes 655376 | tf_op jit(solution)/shard_map/reduce_scatter | solution.py:130
  588.5 1.8 convert_element_type.64
  590.4 4.7 copy.56
  595.1 28.0 %all-gather.8.cloned.1.call-done = bf16[128,5120]{1,0:T(8,128)(2,1)} async-done(((bf16[128,1280]{1,0:T(8,128)(2,1)}), bf16[128,5120]{1,0:T(8,128)(2,1)}) %all-gather.8.cloned.1.call-update) | async-done | bytes 1310736 | tf_op jit(solution)/shard_map/all_gather | solution.py:136
  623.1 2.5 copy.96
  (51 shorter events, 4.6 us)
Async XLA Ops:
  7.2 42.5 %copy-start = (bf16[4,32,5120]{2,1,0:T(8,128)(2,1)S(1)}, bf16[4,32,5120]{2,1,0:T(8,128)(2,1)}, u32[]{:S(2)}) copy-start(bf16[4,32,5120]{2,1,0:T(8,128)(2,1)} %param.19) | copy-start | bytes 3932164
  7.2 0.8 copy-start.7
  7.2 362.0 %all-gather.6.cloned.1.call-start = ((), (), s32[]{:S(2)}) async-start(), calls=%async_computation.4 | async-start | bytes 26214400 | tf_op jit(solution)/shard_map/all_gather | solution.py:85
  7.9 413.4 %all-gather.4.cloned.1.call-start = ((), (), s32[]{:S(2)}) async-start(), calls=%async_computation.3 | async-start | bytes 1638400 | tf_op jit(solution)/shard_map/all_gather | solution.py:128
  56.8 1.7 copy-start.5
  58.6 3.9 copy-start.2
  64.0 1.9 copy-start.4
  65.9 2.2 copy-start.3
  68.2 2.7 copy-start.6
  70.9 443.9 %reduce-scatter.7.cloned.1.call-start = ((), (), s32[]{:S(2)}) async-start(), calls=%async_computation.7 | async-start | bytes 14745600
  423.9 100.5 %all-to-all-start = ((bf16[128,8,640]{2,0,1:T(8,128)(2,1)}), bf16[128,8,640]{2,0,1:T(8,128)(2,1)S(1)}, u32[]{:S(2)}, u32[]{:S(2)}) async-start(bf16[128,8,640]{2,0,1:T(8,128)(2,1)} %bitcast.71), calls=%async_computation | async-start | bytes 2621440 | tf_op jit(solution)/shard_map/all_to_all | solution.py:129
  427.5 161.0 %reduce-scatter.5.cloned.1.call-start = ((), (), s32[]{:S(2)}) async-start(), calls=%async_computation.5 | async-start | bytes 5898240 | tf_op jit(solution)/shard_map/reduce_scatter | solution.py:130
  531.9 91.2 %all-gather.8.cloned.1.call-start = ((), (), s32[]{:S(2)}) async-start(), calls=%async_computation.6 | async-start | bytes 1638400 | tf_op jit(solution)/shard_map/all_gather | solution.py:136
  590.4 35.1 %copy-start.1 = (bf16[4,32,5120]{2,1,0:T(8,128)(2,1)S(1)}, bf16[4,32,5120]{2,1,0:T(8,128)(2,1)}, u32[]{:S(2)}) copy-start(bf16[4,32,5120]{2,1,0:T(8,128)(2,1)} %param.19) | copy-start | bytes 3932164
Sparse Core Ops, SparseCore 0:
  9.6 359.5 all-gather.5
  371.3 31.0 all-gather.3
  421.5 93.2 reduce-scatter.6
  532.0 56.5 reduce-scatter.4
  590.5 32.5 all-gather.7
where the time goes:
time: 634 us; the launch traced here: 632 us
  waiting for transfers between devices  446 us (70%)
  local copies, waits for them, and re-layouts  89.8 us (14%)
  matrix products  57.3 us (9%)
  between operations  14 us (2%)
  other arithmetic  11.4 us (2%)
  blocking collectives  9.6 us (2%)
    all_gather x1, waiting for transfers between devices, per_device(): features = lax.all_gather(context, 'tp', axis=1, tiled=True)  288 us
    unnamed x6, waiting for transfers between devices  73.3 us
    unnamed x24, local copies, waits for them, and re-layouts  61.9 us
    reduce_scatter x1, waiting for transfers between devices, per_device(): lax.psum_scatter(jnp.dot(feature_rows, weight, preferred_element_type=jnp...  56.6 us
    dot_general x1, matrix products, per_device(): lax.dot_general(features, scaled, (((0,), (0,)), ((), ())), preferred_ele...  34.5 us
    all_gather x1, waiting for transfers between devices, per_device(): lax.all_gather(own_columns.astype(jnp.bfloat16), 'tp', axis=1, tiled=True)  28 us
  transfers between devices with their start and end apart: 6, of which 4 were waited for; matrix products, arithmetic and copies ran while one was open for 23% of the time, Pallas kernels for 0%

commit v1 on v0

--- a/solution.py
+++ b/solution.py
@@ -82,7 +82,8 @@
         token_local * replicas
     )
     scaled = (out_grad.astype(jnp.float32) * per_token[:, None]).astype(jnp.bfloat16)
-    features = lax.all_gather(context, "tp", axis=1, tiled=True)
+    back = lax.all_gather(context, "tp")
+    features = jnp.concatenate(back, axis=1)
     gradient = lax.psum_scatter(
         lax.dot_general(
             features, scaled, (((0,), (0,)), ((), ())), preferred_element_type=jnp.float32

time: 634 us -> 663 us (1.046)
  local copies, waits for them, and re-layouts: 89.8 us -> 117 us
    reshape x0 -> x1, local copies, waits for them, and re-layouts: none -> 27.2 us  [per_device(): features = jnp.concatenate(back, axis=1)]
  transfers between devices with their start and end apart: 6 -> 6, of which waited for: 4 -> 4; matrix products, arithmetic and copies ran while one was open for 23% -> 26% of each run, Pallas kernels for 0% -> 0%
where the time goes in v1:
time: 663 us; the launch traced here: 661 us
  waiting for transfers between devices  446 us (67%)
  local copies, waits for them, and re-layouts  117 us (18%)
  matrix products  58.5 us (9%)
  between operations  14 us (2%)
  other arithmetic  11.4 us (2%)
  blocking collectives  9.62 us (1%)
    all_gather x1, waiting for transfers between devices, per_device(): back = lax.all_gather(context, 'tp')  288 us
    unnamed x6, waiting for transfers between devices  72.7 us
    unnamed x24, local copies, waits for them, and re-layouts  62.2 us
    reduce_scatter x1, waiting for transfers between devices, per_device(): lax.psum_scatter(jnp.dot(feature_rows, weight, preferred_element_type=jnp...  56.6 us
    dot_general x1, matrix products, per_device(): lax.dot_general(features, scaled, (((0,), (0,)), ((), ())), preferred_ele...  35.7 us
    all_gather x1, waiting for transfers between devices, per_device(): lax.all_gather(own_columns.astype(jnp.bfloat16), 'tp', axis=1, tiled=True)  28 us
    reshape x1, local copies, waits for them, and re-layouts, per_device(): features = jnp.concatenate(back, axis=1)  27.2 us
  transfers between devices with their start and end apart: 6, of which 4 were waited for; matrix products, arithmetic and copies ran while one was open for 26% of the time, Pallas kernels for 0%

profile of v1, /device:TPU:0, one launch (start us, length us, event | category | flops | bytes accessed | tf_op | source)
XLA Modules:
  0.0 660.5 jit_solution(18140882096426742484)
XLA Ops:
  8.1 4.4 copy.82
  12.5 4.5 copy.87
  17.0 7.3 %reshape.137 = bf16[32,256,2,128]{3,2,1,0:T(2,128)(2,1)} reshape(bf16[32,256,256]{2,1,0:T(8,128)(2,1)} %param.23) | data formatting | bytes 8388608 | tf_op jit(solution)/shard_map/reshape | solution.py:124
  24.3 7.2 %reshape.138 = bf16[32,256,2,128]{3,2,1,0:T(2,128)(2,1)} reshape(bf16[32,256,256]{2,1,0:T(8,128)(2,1)} %param.24) | data formatting | bytes 8388608 | tf_op jit(solution)/shard_map/reshape | solution.py:125
  31.5 17.8 %copy.58 = bf16[5120,1280]{0,1:T(8,128)(2,1)} copy(bf16[5120,1280]{1,0:T(8,128)(2,1)} %param.20) | data formatting | bytes 26214400 | tf_op args[7]
  49.6 7.2 %fusion.27 = f32[4,32,10,128]{3,1,2,0:T(8,128)S(1)} fusion(bf16[10,128,5120,1]{2,1,0,3:T(8,128)(2,1)} %bitcast.79, bf16[4,32,5120]{2,1,0:T(8,128)(2,1)S(1)} %copy-done), kind=kOutput, calls=%fused_computation.34 | convolution fusion | flops 1677721600 | bytes 15073280 | tf_op jit(solution)/shard_map/dot_general | solution.py:107
  57.5 1.1 copy-done.5
  59.9 2.6 fusion.55
  62.4 1.6 bitcast_reduce_fusion
  64.6 1.3 fusion.16
  66.0 1.0 fusion.37
  68.2 1.5 fusion.29
  69.7 1.1 reshape.139
  70.9 9.6 %psum.7 = s32[8]{0:T(128)S(1)} all-reduce(s32[8]{0:T(128)S(1)} %reduce_sum.29), channel_id=1, replica_groups=mesh['rep'=8,'tp'=4] {'rep'}, use_global_device_ids=true, to_apply=%region_5.6 | all-reduce | flops 8 | bytes 64 | tf_op jit(solution)/shard_map/psum | solution.py:77
  80.9 288.3 %all-gather.9.cloned.1.call-done = bf16[8192,1280]{1,0:T(8,128)(2,1)} async-done(((bf16[2048,1280]{1,0:T(8,128)(2,1)}), bf16[8192,1280]{1,0:T(8,128)(2,1)}) %all-gather.9.cloned.1.call-update) | async-done | bytes 20971536 | tf_op jit(solution)/shard_map/all_gather | solution.py:85
  369.2 27.2 %copy.71 = bf16[2048,4,1280]{0,2,1:T(8,128)(2,1)} copy(bf16[2048,4,1280]{2,0,1:T(8,128)(2,1)} %bitcast.76) | data formatting | bytes 41943040 | tf_op jit(solution)/shard_map/reshape | solution.py:86
  396.4 35.7 %fusion = bf16[5120,1280]{0,1:T(8,128)(2,1)} fusion(bf16[2048,5120]{0,1:T(8,128)(2,1)} %bitcast.77, bf16[2048,1280]{1,0:T(8,128)(2,1)} %param.14, f32[2048]{0:T(1024)S(1)} %div.60), kind=kOutput, calls=%fused_computation.1 | convolution fusion | flops 26857963520 | bytes 39329792 | tf_op jit(solution)/shard_map/dot_general | solution.py:88
  432.1 17.6 %copy.90 = bf16[5120,1280]{1,0:T(8,128)(2,1)} copy(bf16[5120,1280]{0,1:T(8,128)(2,1)} %fusion) | data formatting | bytes 26214400
  449.8 2.5 copy.112
  452.3 3.7 all-to-all-start
  456.3 5.1 copy.73
  461.3 5.2 copy.69
  466.5 4.7 copy.72
  471.2 72.0 %reduce-scatter.7.cloned.1.call-done = bf16[640,1280]{1,0:T(8,128)(2,1)} async-done(((bf16[5120,1280]{1,0:T(8,128)(2,1)}), bf16[640,1280]{1,0:T(8,128)(2,1)}) %reduce-scatter.7.cloned.1.call-update) | async-done | bytes 1638416
  543.2 2.8 copy.91
  546.0 6.7 %fusion.8 = f32[640,1280]{0,1:T(8,128)} fusion(bf16[640,1280]{0,1:T(8,128)(2,1)S(1)} %copy.91, f32[640,1280]{0,1:T(8,128)} %copy.72, f32[640,1280]{0,1:T(8,128)} %copy.69), kind=kLoop, calls=%fused_computation.12 | loop fusion | flops 9830400 | bytes 11468800 | tf_op jit(solution)/shard_map/div | solution.py:98
  552.8 7.5 %fusion.14 = f32[1024,1280]{1,0:T(8,128)} fusion(bf16[1024,640]{1,0:T(8,128)(2,1)S(1)} %bitcast.80, f32[640,1280]{0,1:T(8,128)} %copy.73, f32[640,1280]{0,1:T(8,128)} %fusion.8), kind=kOutput, calls=%fused_computation.23 | convolution fusion | flops 1680179200 | bytes 13107200 | tf_op jit(solution)/shard_map/dot_general | solution.py:132
  560.3 56.6 %reduce-scatter.5.cloned.1.call-done = f32[128,1280]{1,0:T(8,128)} async-done(((f32[1024,1280]{1,0:T(8,128)}), f32[128,1280]{1,0:T(8,128)}) %reduce-scatter.5.cloned.1.call-update) | async-done | bytes 655376 | tf_op jit(solution)/shard_map/reduce_scatter | solution.py:131
  617.0 1.8 convert_element_type.64
  618.9 4.7 copy.74
  623.5 28.0 %all-gather.7.cloned.1.call-done = bf16[128,5120]{1,0:T(8,128)(2,1)} async-done(((bf16[128,1280]{1,0:T(8,128)(2,1)}), bf16[128,5120]{1,0:T(8,128)(2,1)}) %all-gather.7.cloned.1.call-update) | async-done | bytes 1310736 | tf_op jit(solution)/shard_map/all_gather | solution.py:137
  651.5 2.5 copy.114
  (52 shorter events, 5.8 us)
Async XLA Ops:
  7.2 42.5 %copy-start = (bf16[4,32,5120]{2,1,0:T(8,128)(2,1)S(1)}, bf16[4,32,5120]{2,1,0:T(8,128)(2,1)}, u32[]{:S(2)}) copy-start(bf16[4,32,5120]{2,1,0:T(8,128)(2,1)} %param.19) | copy-start | bytes 3932164
  7.2 0.8 copy-start.7
  7.2 362.0 %all-gather.9.cloned.1.call-start = ((), (), s32[]{:S(2)}) async-start(), calls=%async_computation.6 | async-start | bytes 26214400 | tf_op jit(solution)/shard_map/all_gather | solution.py:85
  7.9 441.9 %all-gather.5.cloned.1.call-start = ((), (), s32[]{:S(2)}) async-start(), calls=%async_computation.3 | async-start | bytes 1638400 | tf_op jit(solution)/shard_map/all_gather | solution.py:129
  56.8 1.7 copy-start.5
  58.6 3.9 copy-start.2
  64.0 1.9 copy-start.4
  65.9 2.2 copy-start.3
  68.2 2.7 copy-start.6
  70.9 472.3 %reduce-scatter.7.cloned.1.call-start = ((), (), s32[]{:S(2)}) async-start(), calls=%async_computation.7 | async-start | bytes 14745600
  452.3 100.5 %all-to-all-start = ((bf16[128,8,640]{2,0,1:T(8,128)(2,1)}), bf16[128,8,640]{2,0,1:T(8,128)(2,1)S(1)}, u32[]{:S(2)}, u32[]{:S(2)}) async-start(bf16[128,8,640]{2,0,1:T(8,128)(2,1)} %bitcast.75), calls=%async_computation | async-start | bytes 2621440 | tf_op jit(solution)/shard_map/all_to_all | solution.py:130
  456.0 161.0 %reduce-scatter.5.cloned.1.call-start = ((), (), s32[]{:S(2)}) async-start(), calls=%async_computation.4 | async-start | bytes 5898240 | tf_op jit(solution)/shard_map/reduce_scatter | solution.py:131
  560.3 91.2 %all-gather.7.cloned.1.call-start = ((), (), s32[]{:S(2)}) async-start(), calls=%async_computation.5 | async-start | bytes 1638400 | tf_op jit(solution)/shard_map/all_gather | solution.py:137
  618.9 35.1 %copy-start.1 = (bf16[4,32,5120]{2,1,0:T(8,128)(2,1)S(1)}, bf16[4,32,5120]{2,1,0:T(8,128)(2,1)}, u32[]{:S(2)}) copy-start(bf16[4,32,5120]{2,1,0:T(8,128)(2,1)} %param.19) | copy-start | bytes 3932164
Sparse Core Ops, SparseCore 0:
  9.6 359.5 all-gather.8
  371.3 31.0 all-gather.4
  449.9 93.2 reduce-scatter.6
  560.4 56.5 reduce-scatter.4
  619.0 32.5 all-gather.6
